TPU v7x, 256 devices: a whole 4x4x8 slice. The times are simulated.
256 devices in a mesh: src: 64 (over z_hi, x, y, core), rcv: 4 (over z_lo).
Axes of the slice: x: 4, y: 4, z: 8 (z_hi: 2, z_lo: 4; z = z_hi * 4 + z_lo), core: 2. Of those that a mesh axis runs over, the one named last changes fastest.
Arguments:
- src_spec: bfloat16 [2, 16, 256, 4096], P(None, None, 'rcv', 'src'), may hold values from -6 to 6
- rcv_spec: bfloat16 [2, 16, 256, 1024], P(None, None, 'src', 'rcv'), may hold values from -6 to 6
- lag_table: int32 [16, 8192], replicated, may hold values from 0 to 511
- src_pos: int32 [4096], P('src'), may hold values from 0 to 8191
- rcv_pos: int32 [1024], P('rcv'), may hold values from 0 to 8191
Outputs:
- panel_src: float32 [16, 2, 4096, 256], P(None, None, ('src', 'rcv'))
- panel_rcv: float32 [16, 2, 256, 1024], P(None, None, 'src', 'rcv')
All inputs are finite; a program needn't handle non-finite values.
Results may differ from a plain program's by a relative error of at most 0.0035.
Values may be sent and summed in bfloat16 or wider, within the bound.
A program may use at most 64 MiB of HBM per device.

v0:
```python
import math
import jax
import jax.numpy as jnp
from jax import lax
from jax.sharding import PartitionSpec as P

WIN = 8
SEGS = 2


def phase_table(freqs, lags, n_freq):
    index_mod = freqs[:, None, None] * jnp.transpose(lags)[None, :, :] % (2 * n_freq)
    angles = index_mod.astype(jnp.float32) * (math.pi / n_freq)
    return (jnp.cos(angles), jnp.sin(angles))


def cross_block(src_block, rcv_block):
    block_width = src_block.shape[2]
    src_five = src_block.reshape(2, SEGS, WIN, block_width, src_block.shape[3])
    rcv_five = rcv_block.reshape(2, SEGS, WIN, block_width, rcv_block.shape[3])
    swapped = jnp.stack([src_five[1], -src_five[0]])
    real_part = jnp.einsum(
        "cgwfs,cgwfr->gfsr", src_five, rcv_five, preferred_element_type=jnp.float32
    )
    imag_part = jnp.einsum(
        "cgwfs,cgwfr->gfsr", swapped, rcv_five, preferred_element_type=jnp.float32
    )
    floor_mod = jnp.maximum(jnp.sqrt(real_part * real_part + imag_part * imag_part), 1.0)
    stacked_re = (jnp.sum(real_part / floor_mod, axis=0) / SEGS).astype(jnp.bfloat16)
    stacked_im = (jnp.sum(imag_part / floor_mod, axis=0) / SEGS).astype(jnp.bfloat16)
    return (stacked_re, stacked_im)


def source_slant(stacked_re, stacked_im, rcv_cos, rcv_sin, src_cos, src_sin, factor):
    left_op = jnp.concatenate([stacked_re, stacked_im], axis=2)
    cos_b = rcv_cos.astype(jnp.bfloat16)
    sin_b = rcv_sin.astype(jnp.bfloat16)
    upper_half = jnp.concatenate([cos_b, sin_b], axis=2)
    bottom = jnp.concatenate([-sin_b, cos_b], axis=2)
    right_op = jnp.concatenate([upper_half, bottom], axis=1)
    sums = jnp.einsum("fsk,fkq->fsq", left_op, right_op, preferred_element_type=jnp.float32)
    n_slow = rcv_cos.shape[2]
    sum_re = sums[:, :, :n_slow]
    sum_im = sums[:, :, n_slow:]
    panel_re = (sum_re * src_cos + sum_im * src_sin) * factor
    panel_im = (sum_im * src_cos - sum_re * src_sin) * factor
    return jnp.transpose(jnp.stack([panel_re, panel_im]), (3, 0, 2, 1))


def receiver_right(src_cos_b, src_sin_b):
    upper_half = jnp.concatenate([src_cos_b, -src_sin_b], axis=2)
    bottom = jnp.concatenate([src_sin_b, src_cos_b], axis=2)
    return jnp.concatenate([upper_half, bottom], axis=1)


def receiver_sums(left_op, right_op):
    return jnp.einsum("fkr,fkq->fqr", left_op, right_op, preferred_element_type=jnp.float32)


def receiver_outer(sums, rcv_cos, rcv_sin, factor):
    n_slow = rcv_cos.shape[2]
    cos_t = jnp.transpose(rcv_cos, (0, 2, 1))
    sin_t = jnp.transpose(rcv_sin, (0, 2, 1))
    sum_re = sums[:, :n_slow, :]
    sum_im = sums[:, n_slow:, :]
    panel_re = (sum_re * cos_t - sum_im * sin_t) * factor
    panel_im = (sum_re * sin_t + sum_im * cos_t) * factor
    return jnp.transpose(jnp.stack([panel_re, panel_im]), (2, 0, 1, 3))


def per_device(src_spec, rcv_spec, lag_table, src_pos, rcv_pos):
    src_full = lax.all_gather(src_spec, "rcv", axis=2, tiled=True)
    n_freq = src_full.shape[2]
    src_dev = src_full.shape[3]
    rcv_dev = rcv_spec.shape[3]
    n_slow = lag_table.shape[0]
    n_src = lax.axis_size("src")
    n_rcv = lax.axis_size("rcv")
    src_factor = 1.0 / math.sqrt(rcv_dev * n_rcv)
    rcv_factor = 1.0 / math.sqrt(src_dev * n_src)
    lag_src = jnp.take(lag_table, src_pos, axis=1)
    lag_rcv = jnp.take(lag_table, rcv_pos, axis=1)
    src_init = jnp.zeros((n_slow, 2, src_dev, n_freq), jnp.float32)
    other_init = jnp.zeros((n_slow, 2, n_freq, rcv_dev), jnp.float32)
    shard_piece = lax.all_gather(rcv_spec, "src", axis=2, tiled=True)
    block_width = math.gcd(shard_piece.shape[2], 16)

    def inner(turn_index, totals):
        offset = turn_index * block_width
        freqs = offset + jnp.arange(block_width, dtype=jnp.int32)
        src_block = lax.dynamic_slice_in_dim(src_full, offset, block_width, 2)
        rcv_block = lax.dynamic_slice_in_dim(shard_piece, offset, block_width, 2)
        stacked_re, stacked_im = cross_block(src_block, rcv_block)
        rcv_cos, rcv_sin = phase_table(freqs, lag_rcv, n_freq)
        src_cos, src_sin = phase_table(freqs, lag_src, n_freq)
        src_part = source_slant(
            stacked_re, stacked_im, rcv_cos, rcv_sin, src_cos, src_sin, src_factor
        )
        src_total = lax.dynamic_update_slice_in_dim(totals[0], src_part, offset, 3)
        left_op = jnp.concatenate([stacked_re, stacked_im], axis=1)
        right_op = receiver_right(src_cos.astype(jnp.bfloat16), src_sin.astype(jnp.bfloat16))
        rcv_part = receiver_outer(receiver_sums(left_op, right_op), rcv_cos, rcv_sin, rcv_factor)
        other = lax.dynamic_update_slice_in_dim(totals[1], rcv_part, offset, 2)
        return (src_total, other)

    src_total, other = lax.fori_loop(
        0, shard_piece.shape[2] // block_width, inner, (src_init, other_init)
    )
    panel_src = lax.psum_scatter(src_total, "rcv", scatter_dimension=2, tiled=True)
    panel_rcv = lax.psum_scatter(other, "src", scatter_dimension=2, tiled=True)
    return (panel_src, panel_rcv)


def solution(mesh):
    placed = (P(None, None, "rcv", "src"), P(None, None, "src", "rcv"), P(), P("src"), P("rcv"))
    return jax.shard_map(
        per_device,
        mesh=mesh,
        in_specs=placed,
        out_specs=(P(None, None, ("src", "rcv"), None), P(None, None, "src", "rcv")),
        check_vma=False,
    )
```

profile of v0, /device:TPU:1, one launch (start us, length us, event | category | flops | bytes accessed | tf_op | source)
XLA Modules:
  0.0 853.7 jit_solution(8564354730002031349)
XLA Ops:
  9.5 3.5 copy.30
  13.0 2.8 gather_fusion.1
  15.9 2.9 gather_fusion
  19.1 44.0 %all-gather.3.cloned.1.call-done = bf16[2,16,256,64]{3,2,1,0:T(8,128)(2,1)} async-done(((bf16[2,16,64,64]{3,2,1,0:T(8,128)(2,1)}), bf16[2,16,256,64]{3,2,1,0:T(8,128)(2,1)}) %all-gather.3.cloned.1.call-update) | async-done | bytes 1048592 | tf_op jit(solution)/shard_map/all_gather | solution.py:72
  63.1 97.3 %all-gather.5.cloned.1.call-done = bf16[2,16,256,256]{3,1,0,2:T(8,128)(2,1)} async-done(((bf16[2,16,4,256]{3,1,0,2:T(8,128)(2,1)}), bf16[2,16,256,256]{3,1,0,2:T(8,128)(2,1)}) %all-gather.5.cloned.1.call-update) | async-done | bytes 4194320 | tf_op jit(solution)/shard_map/all_gather | solution.py:85
  162.6 4.3 broadcast_in_dim.41.clone
  166.9 212.6 %while.17 = (s32[]{:T(128)}, f32[16,2,64,256]{2,0,3,1:T(8,128)}, f32[16,2,256,256]{3,0,1,2:T(8,128)}, bf16[2,16,256,64]{3,2,1,0:T(8,128)(2,1)}, bf16[2,16,256,25...) while((s32[]{:T(128)}, f32[16,2,64,256]{2,0,3,1:T(8,128)}, ...), condition=%wide.region_3.4_spmd, body=%wide.region_0.3_spmd.sunk | while | flops 116801552 | bytes 17031760 | solution.py:106
  173.2 2.5 fusion.77
  186.5 2.5 fusion.77
  199.8 2.5 fusion.77
  213.1 2.5 fusion.77
  226.4 2.5 fusion.77
  239.6 2.5 fusion.77
  252.9 2.5 fusion.77
  266.2 2.5 fusion.77
  279.5 2.5 fusion.77
  306.1 2.5 fusion.77
  332.6 2.5 fusion.77
  345.9 2.5 fusion.77
  359.2 2.5 fusion.77
  372.5 2.5 fusion.77
  379.6 3.8 copy.35
  383.5 410.5 %reduce-scatter.5.cloned.1.call-done = f32[16,2,4,256]{3,0,1,2:T(8,128)} async-done(((f32[16,2,256,256]{3,0,1,2:T(8,128)}), f32[16,2,4,256]{3,0,1,2:T(8,128)}) %reduce-scatter.5.cloned.1.call-update) | async-done | bytes 131088 | tf_op jit(solution)/shard_map/reduce_scatter | solution.py:110
  795.6 51.6 %reduce-scatter.3.cloned.1.call-done = f32[16,2,16,256]{3,2,1,0:T(8,128)} async-done(((f32[16,2,64,256]{3,2,1,0:T(8,128)}), f32[16,2,16,256]{3,2,1,0:T(8,128)}) %reduce-scatter.3.cloned.1.call-update) | async-done | bytes 524304 | tf_op jit(solution)/shard_map/reduce_scatter | solution.py:109
  (283 shorter events, 182.9 us)
Async XLA Ops:
  7.2 5.9 copy-start.1
  7.2 8.7 %copy-start = (s32[256]{0:T(256)S(1)}, s32[256]{0:T(256)}, u32[]{:S(2)}) copy-start(s32[256]{0:T(256)} %param.11) | copy-start | bytes 3076
  7.2 55.9 %all-gather.3.cloned.1.call-start = ((), (), s32[]{:S(2)}) async-start(), calls=%async_computation.2 | async-start | bytes 2621440 | tf_op jit(solution)/shard_map/all_gather | solution.py:72
  7.9 152.5 %all-gather.5.cloned.1.call-start = ((), (), s32[]{:S(2)}) async-start(), calls=%async_computation.3 | async-start | bytes 4259840 | tf_op jit(solution)/shard_map/all_gather | solution.py:85
  9.5 784.5 %reduce-scatter.5.cloned.1.call-start = ((), (), s32[]{:S(2)}) async-start(), calls=%async_computation.5 | async-start | bytes 8519680 | tf_op jit(solution)/shard_map/reduce_scatter | solution.py:110
  379.6 467.6 %reduce-scatter.3.cloned.1.call-start = ((), (), s32[]{:S(2)}) async-start(), calls=%async_computation.4 | async-start | bytes 2621440 | tf_op jit(solution)/shard_map/reduce_scatter | solution.py:109
Sparse Core Ops, SparseCore 0:
  9.8 53.2 all-gather.2
  67.4 93.0 all-gather.4
  379.7 414.1 reduce-scatter.4
  796.9 50.2 reduce-scatter.2
where the time goes:
time: 856 us; the launch traced here: 854 us
  waiting for transfers between devices  604 us (71%)
  other arithmetic  122 us (14%)
  matrix products  74.5 us (9%)
  local copies, waits for them, and re-layouts  38.2 us (4%)
  between operations  13.8 us (2%)
    reduce_scatter x1, waiting for transfers between devices, per_device(): panel_rcv = lax.psum_scatter(other, 'src', scatter_dimension=2, tiled=True)  410 us
    all_gather x1, waiting for transfers between devices, per_device(): shard_piece = lax.all_gather(rcv_spec, 'src', axis=2, tiled=True)  97.3 us
    reduce_scatter x1, waiting for transfers between devices, per_device(): lax.psum_scatter(src_total, 'rcv', scatter_dimension=2, tiled=True)  51.6 us
    all_gather x1, waiting for transfers between devices, per_device(): src_full = lax.all_gather(src_spec, 'rcv', axis=2, tiled=True)  44 us
    dot_general x16, matrix products, cross_block(): jnp.einsum('cgwfs,cgwfr->gfsr', swapped, rcv_five, preferred_element_type...  40 us
    dot_general x16, matrix products, cross_block(): jnp.einsum('cgwfs,cgwfr->gfsr', src_five, rcv_five, preferred_element_typ...  22.9 us
    another operation x16, other arithmetic, receiver_outer(): return jnp.transpose(jnp.stack([panel_re, panel_im]), (2, 0, 1, 3))  20.8 us
    convert_element_type x16, other arithmetic, source_slant(): sin_b = rcv_sin.astype(jnp.bfloat16)  20.1 us
  transfers between devices with their start and end apart: 4, of which 4 were waited for; matrix products, arithmetic and copies ran while one was open for 2% of the time, Pallas kernels for 0%

commit v1 on v0

--- a/solution.py
+++ b/solution.py
@@ -69,7 +69,9 @@
 
 
 def per_device(src_spec, rcv_spec, lag_table, src_pos, rcv_pos):
-    src_full = lax.all_gather(src_spec, "rcv", axis=2, tiled=True)
+    src_full = jnp.concatenate(
+        lax.all_to_all(jnp.stack([src_spec] * lax.axis_size("rcv")), "rcv", 0, 0), axis=2
+    )
     n_freq = src_full.shape[2]
     src_dev = src_full.shape[3]
     rcv_dev = rcv_spec.shape[3]

time: 856 us -> 807 us (0.943)
  waiting for transfers between devices: 604 us -> 542 us
    all_gather x1 -> x0, waiting for transfers between devices: 44 us -> none  [per_device(): src_full = lax.all_gather(src_spec, 'rcv', axis=2, tiled=True)]
    all_gather x1, waiting for transfers between devices: 97.3 us -> 61.9 us  [per_device(): shard_piece = lax.all_gather(rcv_spec, 'src', axis=2, tiled=True)]
    all_to_all x0 -> x1, waiting for transfers between devices: none -> 17.5 us  [per_device(): lax.all_to_all(jnp.stack([src_spec] * lax.axis_size('rcv')), 'rcv', 0, 0)]
  transfers between devices with their start and end apart: 4 -> 4, of which waited for: 4 -> 4; matrix products, arithmetic and copies ran while one was open for 2% -> 3% of each run, Pallas kernels for 0% -> 0%
where the time goes in v1:
time: 807 us; the launch traced here: 804 us
  waiting for transfers between devices  542 us (67%)
  other arithmetic  122 us (15%)
  matrix products  74.6 us (9%)
  local copies, waits for them, and re-layouts  44.6 us (6%)
  between operations  13.8 us (2%)
    reduce_scatter x1, waiting for transfers between devices, per_device(): panel_rcv = lax.psum_scatter(other, 'src', scatter_dimension=2, tiled=True)  411 us
    all_gather x1, waiting for transfers between devices, per_device(): shard_piece = lax.all_gather(rcv_spec, 'src', axis=2, tiled=True)  61.9 us
    reduce_scatter x1, waiting for transfers between devices, per_device(): lax.psum_scatter(src_total, 'rcv', scatter_dimension=2, tiled=True)  51.7 us
    dot_general x16, matrix products, cross_block(): jnp.einsum('cgwfs,cgwfr->gfsr', swapped, rcv_five, preferred_element_type...  40 us
    dot_general x16, matrix products, cross_block(): jnp.einsum('cgwfs,cgwfr->gfsr', src_five, rcv_five, preferred_element_typ...  22.9 us
    another operation x16, other arithmetic, receiver_outer(): return jnp.transpose(jnp.stack([panel_re, panel_im]), (2, 0, 1, 3))  20.8 us
    convert_element_type x16, other arithmetic, source_slant(): sin_b = rcv_sin.astype(jnp.bfloat16)  20.1 us
    all_to_all x1, waiting for transfers between devices, per_device(): lax.all_to_all(jnp.stack([src_spec] * lax.axis_size('rcv')), 'rcv', 0, 0)  17.5 us
  transfers between devices with their start and end apart: 4, of which 4 were waited for; matrix products, arithmetic and copies ran while one was open for 3% of the time, Pallas kernels for 0%

profile of v1, /device:TPU:1, one launch (start us, length us, event | category | flops | bytes accessed | tf_op | source)
XLA Modules:
  0.0 804.3 jit_solution(17791061472061375342)
XLA Ops:
  10.3 2.7 reshape.94
  13.0 6.6 all-to-all-start
  19.6 2.6 copy.45
  22.2 2.8 gather_fusion.1
  25.0 2.9 gather_fusion
  28.3 17.5 %all-to-all-done = bf16[4,2,65536]{2,1,0:T(2,128)(2,1)S(1)} async-done(((bf16[4,2,65536]{2,1,0:T(2,128)(2,1)}), bf16[4,2,65536]{2,1,0:T(2,128)(2,1)S(1)}, u32[]{:S(2)}, u32[]{:S(2)}) %all-to-all-start) | async-done | bytes 1048608 | tf_op jit(solution)/shard_map/all_to_all | solution.py:73
  48.8 61.9 %all-gather.2.cloned.1.call-done = bf16[2,16,256,256]{3,1,0,2:T(8,128)(2,1)} async-done(((bf16[2,16,4,256]{3,1,0,2:T(8,128)(2,1)}), bf16[2,16,256,256]{3,1,0,2:T(8,128)(2,1)}) %all-gather.2.cloned.1.call-update) | async-done | bytes 4194320 | tf_op jit(solution)/shard_map/all_gather | solution.py:87
  112.9 4.3 broadcast_in_dim.41.clone
  117.2 212.7 %while.17 = (s32[]{:T(128)}, f32[16,2,64,256]{2,0,3,1:T(8,128)}, f32[16,2,256,256]{3,0,1,2:T(8,128)}, bf16[2,16,256,64]{3,2,1,0:T(8,128)(2,1)}, bf16[2,16,256,25...) while((s32[]{:T(128)}, f32[16,2,64,256]{2,0,3,1:T(8,128)}, ...), condition=%wide.region_3.4_spmd, body=%wide.region_0.3_spmd.sunk | while | flops 116801552 | bytes 17031760 | solution.py:108
  123.4 2.5 fusion.77
  136.7 2.5 fusion.77
  150.0 2.5 fusion.77
  163.3 2.5 fusion.77
  176.6 2.5 fusion.77
  203.2 2.5 fusion.77
  216.5 2.5 fusion.77
  229.8 2.5 fusion.77
  243.1 2.5 fusion.77
  256.4 2.5 fusion.77
  269.7 2.5 fusion.77
  296.2 2.5 fusion.77
  329.9 3.8 copy.51
  333.8 410.6 %reduce-scatter.5.cloned.1.call-done = f32[16,2,4,256]{3,0,1,2:T(8,128)} async-done(((f32[16,2,256,256]{3,0,1,2:T(8,128)}), f32[16,2,4,256]{3,0,1,2:T(8,128)}) %reduce-scatter.5.cloned.1.call-update) | async-done | bytes 131088 | tf_op jit(solution)/shard_map/reduce_scatter | solution.py:112
  746.0 51.7 %reduce-scatter.3.cloned.1.call-done = f32[16,2,16,256]{3,2,1,0:T(8,128)} async-done(((f32[16,2,64,256]{3,2,1,0:T(8,128)}), f32[16,2,16,256]{3,2,1,0:T(8,128)}) %reduce-scatter.3.cloned.1.call-update) | async-done | bytes 524304 | tf_op jit(solution)/shard_map/reduce_scatter | solution.py:111
  (288 shorter events, 191.8 us)
Async XLA Ops:
  7.2 12.4 %copy-start = (s32[16,8192]{1,0:T(8,128)S(1)}, s32[16,8192]{1,0:T(8,128)}, u32[]{:S(2)}) copy-start(s32[16,8192]{1,0:T(8,128)} %param.9) | copy-start | bytes 1572868
  7.2 103.5 %all-gather.2.cloned.1.call-start = ((), (), s32[]{:S(2)}) async-start(), calls=%async_computation.3 | async-start | bytes 4259840 | tf_op jit(solution)/shard_map/all_gather | solution.py:87
  13.0 9.2 %copy-start.2 = (s32[64]{0:T(128)S(1)}, s32[64]{0:T(128)}, u32[]{:S(2)}) copy-start(s32[64]{0:T(128)} %param.10) | copy-start | bytes 772
  13.0 12.0 %copy-start.1 = (s32[256]{0:T(256)S(1)}, s32[256]{0:T(256)}, u32[]{:S(2)}) copy-start(s32[256]{0:T(256)} %param.11) | copy-start | bytes 3076
  13.0 32.8 %all-to-all-start = ((bf16[4,2,65536]{2,1,0:T(2,128)(2,1)}), bf16[4,2,65536]{2,1,0:T(2,128)(2,1)S(1)}, u32[]{:S(2)}, u32[]{:S(2)}) async-start(bf16[4,2,65536]{2,1,0:T(2,128)(2,1)} %reshape.94), calls=%async_computation | async-start | bytes 2097152 | tf_op jit(solution)/shard_map/all_to_all | solution.py:73
  19.6 724.8 %reduce-scatter.5.cloned.1.call-start = ((), (), s32[]{:S(2)}) async-start(), calls=%async_computation.5 | async-start | bytes 8519680 | tf_op jit(solution)/shard_map/reduce_scatter | solution.py:112
  329.9 467.8 %reduce-scatter.3.cloned.1.call-start = ((), (), s32[]{:S(2)}) async-start(), calls=%async_computation.4 | async-start | bytes 2621440 | tf_op jit(solution)/shard_map/reduce_scatter | solution.py:111
Sparse Core Ops, SparseCore 0:
  12.2 98.3 all-gather.1
  330.0 414.3 reduce-scatter.4
  747.5 50.1 reduce-scatter.2
